TPU v7x, 32 devices: a whole 2x2x4 slice. The times are simulated.
32 devices in a mesh: energy: 4 (over y, x), slab: 8 (over z, core).
Axes of the slice: x: 2, y: 2, z: 4, core: 2. Of those that a mesh axis runs over, the one named last changes fastest.
Arguments:
- left_basis: bfloat16 [8, 768, 768], P('slab'), may hold values from -0.21875 to 0.21875
- right_basis: bfloat16 [8, 768, 768], P('slab'), may hold values from -0.21875 to 0.21875
- potential_index: int32 [8], P('slab'), may hold values from 0 to 7
- levels: float32 [8, 768], replicated, may hold values from 0.8 to 1.25
- energy_values: float32 [64], replicated, may hold values from -0.1 to 0.1
- energy_weights: float32 [64], replicated, may hold values from 0.2 to 5
- energy_index: int32 [16], P('energy'), may hold values from 0 to 63
- left_source: bfloat16 [768, 128], replicated, may hold values from -6 to 6
- right_source: bfloat16 [768, 128], replicated, may hold values from -6 to 6
Outputs:
- density: float32 [8, 768], P('slab')
All inputs are finite; a program needn't handle non-finite values.
Results may differ from a plain program's by a relative error of at most 0.0044.
Values may be sent and summed in bfloat16 or wider, within the bound.
A program may use at most 64 MiB of HBM per device.

v0:
```python
import jax
import jax.numpy as jnp
from jax import lax
from jax.sharding import PartitionSpec as P


def passed_along(block, axis, distance):
    devices = range(lax.axis_size(axis))
    route = [(i - distance, i) for i in devices if i - distance in devices]
    return lax.ppermute(block, axis, route)


def local(
    left_basis,
    right_basis,
    potential_index,
    levels,
    energy_values,
    energy_weights,
    energy_index,
    left_source,
    right_source,
):
    slab_count = left_basis.shape[0]
    energy_count = energy_index.shape[0]
    orbitals = left_basis.shape[1]
    modes = left_source.shape[1]
    chain = lax.axis_size("slab")
    position = lax.axis_index("slab")
    total_energies = energy_count * lax.axis_size("energy")
    grid_ids = jnp.arange(energy_values.shape[0], dtype=jnp.int32)
    picked = (energy_index[:, None] == grid_ids[None, :]).astype(jnp.float32)
    energy = jnp.sum(picked * energy_values[None, :], axis=1)
    weight = jnp.sum(picked * energy_weights[None, :], axis=1) / (total_energies * modes)
    profile_ids = jnp.arange(levels.shape[0], dtype=jnp.int32)
    profile = (potential_index[:, None] == profile_ids[None, :]).astype(jnp.float32)
    slab_levels = jnp.sum(profile[:, :, None] * levels[None], axis=1)
    factors_all = 1.0 / (energy[None, :, None] - slab_levels[:, None, :])
    slot_ids = jnp.arange(energy_count, dtype=jnp.int32)

    def select(slot):
        chosen = (slot_ids == slot).astype(jnp.float32)
        return (jnp.sum(chosen[None, :, None] * factors_all, axis=1), jnp.sum(chosen * weight))

    def contribution(state, scale):
        squared = state.astype(jnp.float32) ** 2
        return scale * jnp.sum(squared, axis=1)

    def sweep_down(state, factors, scale):
        mixed = jnp.dot(right_basis[0], state, preferred_element_type=jnp.float32)
        scaled = (factors[0][:, None] * mixed).astype(jnp.bfloat16)
        state = jnp.dot(left_basis[0], scaled, preferred_element_type=jnp.float32).astype(
            jnp.bfloat16
        )
        parts = [contribution(state, scale)]
        return (state, jnp.stack(parts))

    def sweep_up(state, factors, scale):
        parts = []
        for index in reversed(range(slab_count)):
            mixed = jnp.einsum(
                "wv,wm->vm", left_basis[index], state, preferred_element_type=jnp.float32
            )
            scaled = (factors[index][:, None] * mixed).astype(jnp.bfloat16)
            state = jnp.einsum(
                "wv,wm->vm", right_basis[index], scaled, preferred_element_type=jnp.float32
            ).astype(jnp.bfloat16)
            parts.append(contribution(state, scale))
        return (state, jnp.stack(parts[::-1]))

    def forward_work(turn, incoming, state, density):
        start = jnp.where(position == 0, left_source, incoming)
        slot = turn - position
        factors, scale = select(slot)
        active = (slot >= 0) & (slot < energy_count)

        def forward_run(begin):
            fresh, parts = sweep_down(begin, factors, scale)
            return (fresh, density + parts)

        def forward_rest(begin):
            return (state, density)

        return lax.cond(active, forward_run, forward_rest, start)

    def backward_work(turn, incoming, state, density):
        start = jnp.where(position == chain - 1, right_source, incoming)
        slot = turn - (chain - 1 - position)
        factors, scale = select(slot)
        active = (slot >= 0) & (slot < energy_count)

        def backward_run(begin):
            fresh, parts = sweep_up(begin, factors, scale)
            return (fresh, density + parts)

        def backward_rest(begin):
            return (state, density)

        return lax.cond(active, backward_run, backward_rest, start)

    turns = chain + energy_count - 1
    zero_state = jnp.zeros((orbitals, modes), jnp.bfloat16)
    zero_density = jnp.zeros((slab_count, orbitals), jnp.float32)

    def forward_turn(turn, carry):
        state, density = carry
        incoming = passed_along(state, "slab", 1)
        return forward_work(turn, incoming, state, density)

    def backward_turn(turn, carry):
        state, density = carry
        incoming = passed_along(state, "slab", -1)
        return backward_work(turn, incoming, state, density)

    _, forward_density = lax.fori_loop(0, turns, forward_turn, (zero_state, zero_density))
    _, backward_density = lax.fori_loop(0, turns, backward_turn, (zero_state, zero_density))
    return lax.psum(forward_density + backward_density, "energy")


def solution(mesh):
    placed = (
        P("slab", None, None),
        P("slab", None, None),
        P("slab"),
        P(),
        P(),
        P(),
        P("energy"),
        P(),
        P(),
    )
    return jax.shard_map(
        local, mesh=mesh, in_specs=placed, out_specs=P("slab", None), check_vma=False
    )
```

profile of v0, /device:TPU:24, one launch (start us, length us, event | category | flops | bytes accessed | tf_op | source)
XLA Modules:
  0.0 214.1 jit_solution(8526664352582363796)
XLA Ops:
  2.4 93.5 %while.38 = (s32[]{:T(128)}, bf16[768,128]{0,1:T(8,128)(2,1)S(1)}, f32[1,768]{1,0:T(1,128)S(1)}, s32[]{:T(128)}, pred[]{:T(512)}, /*index=5*/bf16[768,128]{1,0:T...) while((s32[]{:T(128)}, bf16[768,128]{0,1:T(8,128)(2,1)S(1)}, ...), condition=%wide.region_16.17_spmd.clone.clone, body=%wide.region_10.16_spmd.clone.clone.sunk | while | flops 302690304 | bytes 4156900 | solution.py:116
  4.6 3.2 %collective-permute-done.1 = bf16[768,128]{1,0:T(8,128)(2,1)S(1)} collective-permute-done((bf16[768,128]{1,0:T(8,128)(2,1)S(1)}, bf16[768,128]{1,0:T(8,128)(2,1)S(1)}, u32[]{:S(2)}, u32[]{:S(2)}) %collective-permute-start.1) | collective-permute-done | bytes 196640 | tf_op jit(solution)/shard_map/while/body/eval_jaxpr/ppermute | solution.py:10
  7.9 3.8 %collective-permute-start.1 = (bf16[768,128]{1,0:T(8,128)(2,1)S(1)}, bf16[768,128]{1,0:T(8,128)(2,1)S(1)}, u32[]{:S(2)}, u32[]{:S(2)}) collective-permute-start(bf16[768,128]{1,0:T(8,128)(2,1)S(1)} %copy.17), channel_id=1, source_target_pairs={{1,0},{2,1},{3,2},{4,3},{5,4},{6,5},{7,6},{9,8},{10,9},{11,10},{12... | collective-permute-start | bytes 589832 | tf_op jit(solution)/shard_map/while/body/eval_jaxpr/ppermute | solution.py:10
  14.9 3.7 %conditional.9 = ((bf16[768,128]{0,1:T(8,128)(2,1)S(1)}, f32[1,768]{1,0:T(1,128)S(1)})) conditional(s32[]{:T(128)} %convert_element_type.149, (bf16[768,128]{0,1:T(8,128)(2,1)S(1)}, f32[1,768]{1,0:T(1,128)S(1)}) %tuple.128, (s32[4]{0:T(128)S(1)}, pred[]{:T(512)}, bf16[768,128]{1,0:T(8,128)(2,1)}, bf16[768,128]{1,0:T(8,128)(2,1)S(1)}, ...), branch_computations={%region_11.11_spmd, %region_12.15_spmd.clone} | conditional | flops 302690304 | bytes 2976905 | solution.py:99
  23.9 3.7 %conditional.9 = ((bf16[768,128]{0,1:T(8,128)(2,1)S(1)}, f32[1,768]{1,0:T(1,128)S(1)})) conditional(s32[]{:T(128)} %convert_element_type.149, (bf16[768,128]{0,1:T(8,128)(2,1)S(1)}, f32[1,768]{1,0:T(1,128)S(1)}) %tuple.128, (s32[4]{0:T(128)S(1)}, pred[]{:T(512)}, bf16[768,128]{1,0:T(8,128)(2,1)}, bf16[768,128]{1,0:T(8,128)(2,1)S(1)}, ...), branch_computations={%region_11.11_spmd, %region_12.15_spmd.clone} | conditional | flops 302690304 | bytes 2976905 | solution.py:99
  27.7 3.8 %collective-permute-start.1 = (bf16[768,128]{1,0:T(8,128)(2,1)S(1)}, bf16[768,128]{1,0:T(8,128)(2,1)S(1)}, u32[]{:S(2)}, u32[]{:S(2)}) collective-permute-start(bf16[768,128]{1,0:T(8,128)(2,1)S(1)} %copy.17), channel_id=1, source_target_pairs={{1,0},{2,1},{3,2},{4,3},{5,4},{6,5},{7,6},{9,8},{10,9},{11,10},{12... | collective-permute-start | bytes 589832 | tf_op jit(solution)/shard_map/while/body/eval_jaxpr/ppermute | solution.py:10
  34.7 3.7 %conditional.9 = ((bf16[768,128]{0,1:T(8,128)(2,1)S(1)}, f32[1,768]{1,0:T(1,128)S(1)})) conditional(s32[]{:T(128)} %convert_element_type.149, (bf16[768,128]{0,1:T(8,128)(2,1)S(1)}, f32[1,768]{1,0:T(1,128)S(1)}) %tuple.128, (s32[4]{0:T(128)S(1)}, pred[]{:T(512)}, bf16[768,128]{1,0:T(8,128)(2,1)}, bf16[768,128]{1,0:T(8,128)(2,1)S(1)}, ...), branch_computations={%region_11.11_spmd, %region_12.15_spmd.clone} | conditional | flops 302690304 | bytes 2976905 | solution.py:99
  38.6 3.8 %collective-permute-start.1 = (bf16[768,128]{1,0:T(8,128)(2,1)S(1)}, bf16[768,128]{1,0:T(8,128)(2,1)S(1)}, u32[]{:S(2)}, u32[]{:S(2)}) collective-permute-start(bf16[768,128]{1,0:T(8,128)(2,1)S(1)} %copy.17), channel_id=1, source_target_pairs={{1,0},{2,1},{3,2},{4,3},{5,4},{6,5},{7,6},{9,8},{10,9},{11,10},{12... | collective-permute-start | bytes 589832 | tf_op jit(solution)/shard_map/while/body/eval_jaxpr/ppermute | solution.py:10
  45.6 3.7 %conditional.9 = ((bf16[768,128]{0,1:T(8,128)(2,1)S(1)}, f32[1,768]{1,0:T(1,128)S(1)})) conditional(s32[]{:T(128)} %convert_element_type.149, (bf16[768,128]{0,1:T(8,128)(2,1)S(1)}, f32[1,768]{1,0:T(1,128)S(1)}) %tuple.128, (s32[4]{0:T(128)S(1)}, pred[]{:T(512)}, bf16[768,128]{1,0:T(8,128)(2,1)}, bf16[768,128]{1,0:T(8,128)(2,1)S(1)}, ...), branch_computations={%region_11.11_spmd, %region_12.15_spmd.clone} | conditional | flops 302690304 | bytes 2976905 | solution.py:99
  49.5 3.8 %collective-permute-start.1 = (bf16[768,128]{1,0:T(8,128)(2,1)S(1)}, bf16[768,128]{1,0:T(8,128)(2,1)S(1)}, u32[]{:S(2)}, u32[]{:S(2)}) collective-permute-start(bf16[768,128]{1,0:T(8,128)(2,1)S(1)} %copy.17), channel_id=1, source_target_pairs={{1,0},{2,1},{3,2},{4,3},{5,4},{6,5},{7,6},{9,8},{10,9},{11,10},{12... | collective-permute-start | bytes 589832 | tf_op jit(solution)/shard_map/while/body/eval_jaxpr/ppermute | solution.py:10
  56.6 7.5 %collective-permute-start.1 = (bf16[768,128]{1,0:T(8,128)(2,1)S(1)}, bf16[768,128]{1,0:T(8,128)(2,1)S(1)}, u32[]{:S(2)}, u32[]{:S(2)}) collective-permute-start(bf16[768,128]{1,0:T(8,128)(2,1)S(1)} %copy.17), channel_id=1, source_target_pairs={{1,0},{2,1},{3,2},{4,3},{5,4},{6,5},{7,6},{9,8},{10,9},{11,10},{12... | collective-permute-start | bytes 589832 | tf_op jit(solution)/shard_map/while/body/eval_jaxpr/ppermute | solution.py:10
  67.5 3.8 %collective-permute-start.1 = (bf16[768,128]{1,0:T(8,128)(2,1)S(1)}, bf16[768,128]{1,0:T(8,128)(2,1)S(1)}, u32[]{:S(2)}, u32[]{:S(2)}) collective-permute-start(bf16[768,128]{1,0:T(8,128)(2,1)S(1)} %copy.17), channel_id=1, source_target_pairs={{1,0},{2,1},{3,2},{4,3},{5,4},{6,5},{7,6},{9,8},{10,9},{11,10},{12... | collective-permute-start | bytes 589832 | tf_op jit(solution)/shard_map/while/body/eval_jaxpr/ppermute | solution.py:10
  74.7 3.8 %collective-permute-start.1 = (bf16[768,128]{1,0:T(8,128)(2,1)S(1)}, bf16[768,128]{1,0:T(8,128)(2,1)S(1)}, u32[]{:S(2)}, u32[]{:S(2)}) collective-permute-start(bf16[768,128]{1,0:T(8,128)(2,1)S(1)} %copy.17), channel_id=1, source_target_pairs={{1,0},{2,1},{3,2},{4,3},{5,4},{6,5},{7,6},{9,8},{10,9},{11,10},{12... | collective-permute-start | bytes 589832 | tf_op jit(solution)/shard_map/while/body/eval_jaxpr/ppermute | solution.py:10
  81.8 3.8 %collective-permute-start.1 = (bf16[768,128]{1,0:T(8,128)(2,1)S(1)}, bf16[768,128]{1,0:T(8,128)(2,1)S(1)}, u32[]{:S(2)}, u32[]{:S(2)}) collective-permute-start(bf16[768,128]{1,0:T(8,128)(2,1)S(1)} %copy.17), channel_id=1, source_target_pairs={{1,0},{2,1},{3,2},{4,3},{5,4},{6,5},{7,6},{9,8},{10,9},{11,10},{12... | collective-permute-start | bytes 589832 | tf_op jit(solution)/shard_map/while/body/eval_jaxpr/ppermute | solution.py:10
  89.0 3.8 %collective-permute-start.1 = (bf16[768,128]{1,0:T(8,128)(2,1)S(1)}, bf16[768,128]{1,0:T(8,128)(2,1)S(1)}, u32[]{:S(2)}, u32[]{:S(2)}) collective-permute-start(bf16[768,128]{1,0:T(8,128)(2,1)S(1)} %copy.17), channel_id=1, source_target_pairs={{1,0},{2,1},{3,2},{4,3},{5,4},{6,5},{7,6},{9,8},{10,9},{11,10},{12... | collective-permute-start | bytes 589832 | tf_op jit(solution)/shard_map/while/body/eval_jaxpr/ppermute | solution.py:10
  96.0 107.6 %while.37 = (s32[]{:T(128)}, bf16[768,128]{0,1:T(8,128)(2,1)S(1)}, f32[1,768]{1,0:T(1,128)S(1)}, s32[]{:T(128)}, pred[]{:T(512)}, /*index=5*/bf16[768,128]{1,0:T...) while((s32[]{:T(128)}, bf16[768,128]{0,1:T(8,128)(2,1)S(1)}, ...), condition=%wide.region_9.10_spmd.clone.clone, body=%wide.region_3.9_spmd.clone.clone.sunk | while | flops 302690304 | bytes 4156900 | solution.py:115
  98.1 5.2 %collective-permute-done = bf16[768,128]{1,0:T(8,128)(2,1)S(1)} collective-permute-done((bf16[768,128]{1,0:T(8,128)(2,1)S(1)}, bf16[768,128]{1,0:T(8,128)(2,1)S(1)}, u32[]{:S(2)}, u32[]{:S(2)}) %collective-permute-start) | collective-permute-done | bytes 196640 | tf_op jit(solution)/shard_map/while/body/eval_jaxpr/ppermute | solution.py:10
  105.4 5.0 %collective-permute-done = bf16[768,128]{1,0:T(8,128)(2,1)S(1)} collective-permute-done((bf16[768,128]{1,0:T(8,128)(2,1)S(1)}, bf16[768,128]{1,0:T(8,128)(2,1)S(1)}, u32[]{:S(2)}, u32[]{:S(2)}) %collective-permute-start) | collective-permute-done | bytes 196640 | tf_op jit(solution)/shard_map/while/body/eval_jaxpr/ppermute | solution.py:10
  112.6 5.0 %collective-permute-done = bf16[768,128]{1,0:T(8,128)(2,1)S(1)} collective-permute-done((bf16[768,128]{1,0:T(8,128)(2,1)S(1)}, bf16[768,128]{1,0:T(8,128)(2,1)S(1)}, u32[]{:S(2)}, u32[]{:S(2)}) %collective-permute-start) | collective-permute-done | bytes 196640 | tf_op jit(solution)/shard_map/while/body/eval_jaxpr/ppermute | solution.py:10
  119.8 5.0 %collective-permute-done = bf16[768,128]{1,0:T(8,128)(2,1)S(1)} collective-permute-done((bf16[768,128]{1,0:T(8,128)(2,1)S(1)}, bf16[768,128]{1,0:T(8,128)(2,1)S(1)}, u32[]{:S(2)}, u32[]{:S(2)}) %collective-permute-start) | collective-permute-done | bytes 196640 | tf_op jit(solution)/shard_map/while/body/eval_jaxpr/ppermute | solution.py:10
  126.9 5.0 %collective-permute-done = bf16[768,128]{1,0:T(8,128)(2,1)S(1)} collective-permute-done((bf16[768,128]{1,0:T(8,128)(2,1)S(1)}, bf16[768,128]{1,0:T(8,128)(2,1)S(1)}, u32[]{:S(2)}, u32[]{:S(2)}) %collective-permute-start) | collective-permute-done | bytes 196640 | tf_op jit(solution)/shard_map/while/body/eval_jaxpr/ppermute | solution.py:10
  134.1 5.0 %collective-permute-done = bf16[768,128]{1,0:T(8,128)(2,1)S(1)} collective-permute-done((bf16[768,128]{1,0:T(8,128)(2,1)S(1)}, bf16[768,128]{1,0:T(8,128)(2,1)S(1)}, u32[]{:S(2)}, u32[]{:S(2)}) %collective-permute-start) | collective-permute-done | bytes 196640 | tf_op jit(solution)/shard_map/while/body/eval_jaxpr/ppermute | solution.py:10
  141.2 18.0 %collective-permute-done = bf16[768,128]{1,0:T(8,128)(2,1)S(1)} collective-permute-done((bf16[768,128]{1,0:T(8,128)(2,1)S(1)}, bf16[768,128]{1,0:T(8,128)(2,1)S(1)}, u32[]{:S(2)}, u32[]{:S(2)}) %collective-permute-start) | collective-permute-done | bytes 196640 | tf_op jit(solution)/shard_map/while/body/eval_jaxpr/ppermute | solution.py:10
  159.3 3.9 %conditional.8 = ((bf16[768,128]{0,1:T(8,128)(2,1)S(1)}, f32[1,768]{1,0:T(1,128)S(1)})) conditional(s32[]{:T(128)} %convert_element_type.148, (bf16[768,128]{0,1:T(8,128)(2,1)S(1)}, f32[1,768]{1,0:T(1,128)S(1)}) %tuple.125, (s32[4]{0:T(128)S(1)}, pred[]{:T(512)}, bf16[768,128]{1,0:T(8,128)(2,1)S(1)}, bf16[768,128]{1,0:T(8,128)(2,1)S(1)}, ...), branch_computations={%region_4.4_spmd, %region_5.8_spmd.clone} | conditional | flops 302690304 | bytes 2976905 | solution.py:84
  165.3 5.1 %collective-permute-done = bf16[768,128]{1,0:T(8,128)(2,1)S(1)} collective-permute-done((bf16[768,128]{1,0:T(8,128)(2,1)S(1)}, bf16[768,128]{1,0:T(8,128)(2,1)S(1)}, u32[]{:S(2)}, u32[]{:S(2)}) %collective-permute-start) | collective-permute-done | bytes 196640 | tf_op jit(solution)/shard_map/while/body/eval_jaxpr/ppermute | solution.py:10
  170.3 3.9 %conditional.8 = ((bf16[768,128]{0,1:T(8,128)(2,1)S(1)}, f32[1,768]{1,0:T(1,128)S(1)})) conditional(s32[]{:T(128)} %convert_element_type.148, (bf16[768,128]{0,1:T(8,128)(2,1)S(1)}, f32[1,768]{1,0:T(1,128)S(1)}) %tuple.125, (s32[4]{0:T(128)S(1)}, pred[]{:T(512)}, bf16[768,128]{1,0:T(8,128)(2,1)S(1)}, bf16[768,128]{1,0:T(8,128)(2,1)S(1)}, ...), branch_computations={%region_4.4_spmd, %region_5.8_spmd.clone} | conditional | flops 302690304 | bytes 2976905 | solution.py:84
  176.4 5.0 %collective-permute-done = bf16[768,128]{1,0:T(8,128)(2,1)S(1)} collective-permute-done((bf16[768,128]{1,0:T(8,128)(2,1)S(1)}, bf16[768,128]{1,0:T(8,128)(2,1)S(1)}, u32[]{:S(2)}, u32[]{:S(2)}) %collective-permute-start) | collective-permute-done | bytes 196640 | tf_op jit(solution)/shard_map/while/body/eval_jaxpr/ppermute | solution.py:10
  181.4 3.9 %conditional.8 = ((bf16[768,128]{0,1:T(8,128)(2,1)S(1)}, f32[1,768]{1,0:T(1,128)S(1)})) conditional(s32[]{:T(128)} %convert_element_type.148, (bf16[768,128]{0,1:T(8,128)(2,1)S(1)}, f32[1,768]{1,0:T(1,128)S(1)}) %tuple.125, (s32[4]{0:T(128)S(1)}, pred[]{:T(512)}, bf16[768,128]{1,0:T(8,128)(2,1)S(1)}, bf16[768,128]{1,0:T(8,128)(2,1)S(1)}, ...), branch_computations={%region_4.4_spmd, %region_5.8_spmd.clone} | conditional | flops 302690304 | bytes 2976905 | solution.py:84
  187.4 5.0 %collective-permute-done = bf16[768,128]{1,0:T(8,128)(2,1)S(1)} collective-permute-done((bf16[768,128]{1,0:T(8,128)(2,1)S(1)}, bf16[768,128]{1,0:T(8,128)(2,1)S(1)}, u32[]{:S(2)}, u32[]{:S(2)}) %collective-permute-start) | collective-permute-done | bytes 196640 | tf_op jit(solution)/shard_map/while/body/eval_jaxpr/ppermute | solution.py:10
  192.5 3.9 %conditional.8 = ((bf16[768,128]{0,1:T(8,128)(2,1)S(1)}, f32[1,768]{1,0:T(1,128)S(1)})) conditional(s32[]{:T(128)} %convert_element_type.148, (bf16[768,128]{0,1:T(8,128)(2,1)S(1)}, f32[1,768]{1,0:T(1,128)S(1)}) %tuple.125, (s32[4]{0:T(128)S(1)}, pred[]{:T(512)}, bf16[768,128]{1,0:T(8,128)(2,1)S(1)}, bf16[768,128]{1,0:T(8,128)(2,1)S(1)}, ...), branch_computations={%region_4.4_spmd, %region_5.8_spmd.clone} | conditional | flops 302690304 | bytes 2976905 | solution.py:84
  198.5 5.0 %collective-permute-done = bf16[768,128]{1,0:T(8,128)(2,1)S(1)} collective-permute-done((bf16[768,128]{1,0:T(8,128)(2,1)S(1)}, bf16[768,128]{1,0:T(8,128)(2,1)S(1)}, u32[]{:S(2)}, u32[]{:S(2)}) %collective-permute-start) | collective-permute-done | bytes 196640 | tf_op jit(solution)/shard_map/while/body/eval_jaxpr/ppermute | solution.py:10
  203.6 10.5 %psum.7 = f32[1,768]{1,0:T(1,128)} all-reduce(f32[1,768]{1,0:T(1,128)S(1)} %add.52), channel_id=1, replica_groups=mesh['energy'=4,'slab'=8] {'energy'}, use_global_device_ids=true, to_apply=%region_17.18 | all-reduce | flops 768 | bytes 6144 | tf_op jit(solution)/shard_map/psum | solution.py:117
  (140 shorter events, 92.0 us)
Async XLA Ops:
  2.4 93.6 %copy-start = (bf16[768,128]{1,0:T(8,128)(2,1)S(1)}, bf16[768,128]{1,0:T(8,128)(2,1)}, u32[]{:S(2)}) copy-start(bf16[768,128]{1,0:T(8,128)(2,1)} %param.24) | copy-start | bytes 589828
  2.6 5.1 %collective-permute-start.1 = (bf16[768,128]{1,0:T(8,128)(2,1)S(1)}, bf16[768,128]{1,0:T(8,128)(2,1)S(1)}, u32[]{:S(2)}, u32[]{:S(2)}) collective-permute-start(bf16[768,128]{1,0:T(8,128)(2,1)S(1)} %copy.17), channel_id=1, source_target_pairs={{1,0},{2,1},{3,2},{4,3},{5,4},{6,5},{7,6},{9,8},{10,9},{11,10},{12... | collective-permute-start | bytes 589832 | tf_op jit(solution)/shard_map/while/body/eval_jaxpr/ppermute | solution.py:10
  7.9 7.0 %collective-permute-start.1 = (bf16[768,128]{1,0:T(8,128)(2,1)S(1)}, bf16[768,128]{1,0:T(8,128)(2,1)S(1)}, u32[]{:S(2)}, u32[]{:S(2)}) collective-permute-start(bf16[768,128]{1,0:T(8,128)(2,1)S(1)} %copy.17), channel_id=1, source_target_pairs={{1,0},{2,1},{3,2},{4,3},{5,4},{6,5},{7,6},{9,8},{10,9},{11,10},{12... | collective-permute-start | bytes 589832 | tf_op jit(solution)/shard_map/while/body/eval_jaxpr/ppermute | solution.py:10
  18.8 5.1 %collective-permute-start.1 = (bf16[768,128]{1,0:T(8,128)(2,1)S(1)}, bf16[768,128]{1,0:T(8,128)(2,1)S(1)}, u32[]{:S(2)}, u32[]{:S(2)}) collective-permute-start(bf16[768,128]{1,0:T(8,128)(2,1)S(1)} %copy.17), channel_id=1, source_target_pairs={{1,0},{2,1},{3,2},{4,3},{5,4},{6,5},{7,6},{9,8},{10,9},{11,10},{12... | collective-permute-start | bytes 589832 | tf_op jit(solution)/shard_map/while/body/eval_jaxpr/ppermute | solution.py:10
  27.7 7.0 %collective-permute-start.1 = (bf16[768,128]{1,0:T(8,128)(2,1)S(1)}, bf16[768,128]{1,0:T(8,128)(2,1)S(1)}, u32[]{:S(2)}, u32[]{:S(2)}) collective-permute-start(bf16[768,128]{1,0:T(8,128)(2,1)S(1)} %copy.17), channel_id=1, source_target_pairs={{1,0},{2,1},{3,2},{4,3},{5,4},{6,5},{7,6},{9,8},{10,9},{11,10},{12... | collective-permute-start | bytes 589832 | tf_op jit(solution)/shard_map/while/body/eval_jaxpr/ppermute | solution.py:10
  38.6 7.0 %collective-permute-start.1 = (bf16[768,128]{1,0:T(8,128)(2,1)S(1)}, bf16[768,128]{1,0:T(8,128)(2,1)S(1)}, u32[]{:S(2)}, u32[]{:S(2)}) collective-permute-start(bf16[768,128]{1,0:T(8,128)(2,1)S(1)} %copy.17), channel_id=1, source_target_pairs={{1,0},{2,1},{3,2},{4,3},{5,4},{6,5},{7,6},{9,8},{10,9},{11,10},{12... | collective-permute-start | bytes 589832 | tf_op jit(solution)/shard_map/while/body/eval_jaxpr/ppermute | solution.py:10
  49.5 7.0 %collective-permute-start.1 = (bf16[768,128]{1,0:T(8,128)(2,1)S(1)}, bf16[768,128]{1,0:T(8,128)(2,1)S(1)}, u32[]{:S(2)}, u32[]{:S(2)}) collective-permute-start(bf16[768,128]{1,0:T(8,128)(2,1)S(1)} %copy.17), channel_id=1, source_target_pairs={{1,0},{2,1},{3,2},{4,3},{5,4},{6,5},{7,6},{9,8},{10,9},{11,10},{12... | collective-permute-start | bytes 589832 | tf_op jit(solution)/shard_map/while/body/eval_jaxpr/ppermute | solution.py:10
  56.6 10.7 %collective-permute-start.1 = (bf16[768,128]{1,0:T(8,128)(2,1)S(1)}, bf16[768,128]{1,0:T(8,128)(2,1)S(1)}, u32[]{:S(2)}, u32[]{:S(2)}) collective-permute-start(bf16[768,128]{1,0:T(8,128)(2,1)S(1)} %copy.17), channel_id=1, source_target_pairs={{1,0},{2,1},{3,2},{4,3},{5,4},{6,5},{7,6},{9,8},{10,9},{11,10},{12... | collective-permute-start | bytes 589832 | tf_op jit(solution)/shard_map/while/body/eval_jaxpr/ppermute | solution.py:10
  67.5 7.0 %collective-permute-start.1 = (bf16[768,128]{1,0:T(8,128)(2,1)S(1)}, bf16[768,128]{1,0:T(8,128)(2,1)S(1)}, u32[]{:S(2)}, u32[]{:S(2)}) collective-permute-start(bf16[768,128]{1,0:T(8,128)(2,1)S(1)} %copy.17), channel_id=1, source_target_pairs={{1,0},{2,1},{3,2},{4,3},{5,4},{6,5},{7,6},{9,8},{10,9},{11,10},{12... | collective-permute-start | bytes 589832 | tf_op jit(solution)/shard_map/while/body/eval_jaxpr/ppermute | solution.py:10
  74.7 7.0 %collective-permute-start.1 = (bf16[768,128]{1,0:T(8,128)(2,1)S(1)}, bf16[768,128]{1,0:T(8,128)(2,1)S(1)}, u32[]{:S(2)}, u32[]{:S(2)}) collective-permute-start(bf16[768,128]{1,0:T(8,128)(2,1)S(1)} %copy.17), channel_id=1, source_target_pairs={{1,0},{2,1},{3,2},{4,3},{5,4},{6,5},{7,6},{9,8},{10,9},{11,10},{12... | collective-permute-start | bytes 589832 | tf_op jit(solution)/shard_map/while/body/eval_jaxpr/ppermute | solution.py:10
  81.8 7.0 %collective-permute-start.1 = (bf16[768,128]{1,0:T(8,128)(2,1)S(1)}, bf16[768,128]{1,0:T(8,128)(2,1)S(1)}, u32[]{:S(2)}, u32[]{:S(2)}) collective-permute-start(bf16[768,128]{1,0:T(8,128)(2,1)S(1)} %copy.17), channel_id=1, source_target_pairs={{1,0},{2,1},{3,2},{4,3},{5,4},{6,5},{7,6},{9,8},{10,9},{11,10},{12... | collective-permute-start | bytes 589832 | tf_op jit(solution)/shard_map/while/body/eval_jaxpr/ppermute | solution.py:10
  89.0 7.0 %collective-permute-start.1 = (bf16[768,128]{1,0:T(8,128)(2,1)S(1)}, bf16[768,128]{1,0:T(8,128)(2,1)S(1)}, u32[]{:S(2)}, u32[]{:S(2)}) collective-permute-start(bf16[768,128]{1,0:T(8,128)(2,1)S(1)} %copy.17), channel_id=1, source_target_pairs={{1,0},{2,1},{3,2},{4,3},{5,4},{6,5},{7,6},{9,8},{10,9},{11,10},{12... | collective-permute-start | bytes 589832 | tf_op jit(solution)/shard_map/while/body/eval_jaxpr/ppermute | solution.py:10
  96.2 7.2 %collective-permute-start = (bf16[768,128]{1,0:T(8,128)(2,1)S(1)}, bf16[768,128]{1,0:T(8,128)(2,1)S(1)}, u32[]{:S(2)}, u32[]{:S(2)}) collective-permute-start(bf16[768,128]{1,0:T(8,128)(2,1)S(1)} %copy.16), channel_id=1, source_target_pairs={{0,1},{1,2},{2,3},{3,4},{4,5},{5,6},{6,7},{8,9},{9,10},{10,11},{11... | collective-permute-start | bytes 589832 | tf_op jit(solution)/shard_map/while/body/eval_jaxpr/ppermute | solution.py:10
  103.5 7.0 %collective-permute-start = (bf16[768,128]{1,0:T(8,128)(2,1)S(1)}, bf16[768,128]{1,0:T(8,128)(2,1)S(1)}, u32[]{:S(2)}, u32[]{:S(2)}) collective-permute-start(bf16[768,128]{1,0:T(8,128)(2,1)S(1)} %copy.16), channel_id=1, source_target_pairs={{0,1},{1,2},{2,3},{3,4},{4,5},{5,6},{6,7},{8,9},{9,10},{10,11},{11... | collective-permute-start | bytes 589832 | tf_op jit(solution)/shard_map/while/body/eval_jaxpr/ppermute | solution.py:10
  110.7 7.0 %collective-permute-start = (bf16[768,128]{1,0:T(8,128)(2,1)S(1)}, bf16[768,128]{1,0:T(8,128)(2,1)S(1)}, u32[]{:S(2)}, u32[]{:S(2)}) collective-permute-start(bf16[768,128]{1,0:T(8,128)(2,1)S(1)} %copy.16), channel_id=1, source_target_pairs={{0,1},{1,2},{2,3},{3,4},{4,5},{5,6},{6,7},{8,9},{9,10},{10,11},{11... | collective-permute-start | bytes 589832 | tf_op jit(solution)/shard_map/while/body/eval_jaxpr/ppermute | solution.py:10
  117.8 7.0 %collective-permute-start = (bf16[768,128]{1,0:T(8,128)(2,1)S(1)}, bf16[768,128]{1,0:T(8,128)(2,1)S(1)}, u32[]{:S(2)}, u32[]{:S(2)}) collective-permute-start(bf16[768,128]{1,0:T(8,128)(2,1)S(1)} %copy.16), channel_id=1, source_target_pairs={{0,1},{1,2},{2,3},{3,4},{4,5},{5,6},{6,7},{8,9},{9,10},{10,11},{11... | collective-permute-start | bytes 589832 | tf_op jit(solution)/shard_map/while/body/eval_jaxpr/ppermute | solution.py:10
  125.0 7.0 %collective-permute-start = (bf16[768,128]{1,0:T(8,128)(2,1)S(1)}, bf16[768,128]{1,0:T(8,128)(2,1)S(1)}, u32[]{:S(2)}, u32[]{:S(2)}) collective-permute-start(bf16[768,128]{1,0:T(8,128)(2,1)S(1)} %copy.16), channel_id=1, source_target_pairs={{0,1},{1,2},{2,3},{3,4},{4,5},{5,6},{6,7},{8,9},{9,10},{10,11},{11... | collective-permute-start | bytes 589832 | tf_op jit(solution)/shard_map/while/body/eval_jaxpr/ppermute | solution.py:10
  132.1 7.0 %collective-permute-start = (bf16[768,128]{1,0:T(8,128)(2,1)S(1)}, bf16[768,128]{1,0:T(8,128)(2,1)S(1)}, u32[]{:S(2)}, u32[]{:S(2)}) collective-permute-start(bf16[768,128]{1,0:T(8,128)(2,1)S(1)} %copy.16), channel_id=1, source_target_pairs={{0,1},{1,2},{2,3},{3,4},{4,5},{5,6},{6,7},{8,9},{9,10},{10,11},{11... | collective-permute-start | bytes 589832 | tf_op jit(solution)/shard_map/while/body/eval_jaxpr/ppermute | solution.py:10
  139.3 20.0 %collective-permute-start = (bf16[768,128]{1,0:T(8,128)(2,1)S(1)}, bf16[768,128]{1,0:T(8,128)(2,1)S(1)}, u32[]{:S(2)}, u32[]{:S(2)}) collective-permute-start(bf16[768,128]{1,0:T(8,128)(2,1)S(1)} %copy.16), channel_id=1, source_target_pairs={{0,1},{1,2},{2,3},{3,4},{4,5},{5,6},{6,7},{8,9},{9,10},{10,11},{11... | collective-permute-start | bytes 589832 | tf_op jit(solution)/shard_map/while/body/eval_jaxpr/ppermute | solution.py:10
  163.3 7.0 %collective-permute-start = (bf16[768,128]{1,0:T(8,128)(2,1)S(1)}, bf16[768,128]{1,0:T(8,128)(2,1)S(1)}, u32[]{:S(2)}, u32[]{:S(2)}) collective-permute-start(bf16[768,128]{1,0:T(8,128)(2,1)S(1)} %copy.16), channel_id=1, source_target_pairs={{0,1},{1,2},{2,3},{3,4},{4,5},{5,6},{6,7},{8,9},{9,10},{10,11},{11... | collective-permute-start | bytes 589832 | tf_op jit(solution)/shard_map/while/body/eval_jaxpr/ppermute | solution.py:10
  174.4 7.0 %collective-permute-start = (bf16[768,128]{1,0:T(8,128)(2,1)S(1)}, bf16[768,128]{1,0:T(8,128)(2,1)S(1)}, u32[]{:S(2)}, u32[]{:S(2)}) collective-permute-start(bf16[768,128]{1,0:T(8,128)(2,1)S(1)} %copy.16), channel_id=1, source_target_pairs={{0,1},{1,2},{2,3},{3,4},{4,5},{5,6},{6,7},{8,9},{9,10},{10,11},{11... | collective-permute-start | bytes 589832 | tf_op jit(solution)/shard_map/while/body/eval_jaxpr/ppermute | solution.py:10
  185.5 7.0 %collective-permute-start = (bf16[768,128]{1,0:T(8,128)(2,1)S(1)}, bf16[768,128]{1,0:T(8,128)(2,1)S(1)}, u32[]{:S(2)}, u32[]{:S(2)}) collective-permute-start(bf16[768,128]{1,0:T(8,128)(2,1)S(1)} %copy.16), channel_id=1, source_target_pairs={{0,1},{1,2},{2,3},{3,4},{4,5},{5,6},{6,7},{8,9},{9,10},{10,11},{11... | collective-permute-start | bytes 589832 | tf_op jit(solution)/shard_map/while/body/eval_jaxpr/ppermute | solution.py:10
  196.6 7.0 %collective-permute-start = (bf16[768,128]{1,0:T(8,128)(2,1)S(1)}, bf16[768,128]{1,0:T(8,128)(2,1)S(1)}, u32[]{:S(2)}, u32[]{:S(2)}) collective-permute-start(bf16[768,128]{1,0:T(8,128)(2,1)S(1)} %copy.16), channel_id=1, source_target_pairs={{0,1},{1,2},{2,3},{3,4},{4,5},{5,6},{6,7},{8,9},{9,10},{10,11},{11... | collective-permute-start | bytes 589832 | tf_op jit(solution)/shard_map/while/body/eval_jaxpr/ppermute | solution.py:10
where the time goes:
time: 215 us; the launch traced here: 214 us
  waiting for transfers between devices  103 us (48%)
  starting transfers between devices  63 us (29%)
  matrix products  19.5 us (9%)
  other arithmetic  12.4 us (6%)
  blocking collectives  10.5 us (5%)
  local copies, waits for them, and re-layouts  3.61 us (2%)
    ppermute x22, waiting for transfers between devices, passed_along(): return lax.ppermute(block, axis, route)  103 us
    ppermute x22, starting transfers between devices, passed_along(): return lax.ppermute(block, axis, route)  63 us
    psum x1, blocking collectives, local(): return lax.psum(forward_density + backward_density, 'energy')  10.5 us
    dot_general x4, matrix products, sweep_down(): jnp.dot(left_basis[0], scaled, preferred_element_type=jnp.float32)  10.1 us
    dot_general x4, matrix products, sweep_up(): jnp.einsum('wv,wm->vm', right_basis[index], scaled, preferred_element_typ...  9.33 us
    reduce_sum x8, other arithmetic, select(): jnp.sum(chosen * weight)  4.96 us
    mul x8, other arithmetic, contribution(): return scale * jnp.sum(squared, axis=1)  4.91 us
  transfers between devices with their start and end apart: 22, of which 22 were waited for; matrix products, arithmetic and copies ran while one was open for 0% of the time, Pallas kernels for 0%

commit v1 on v0

v1 whole, which is shorter than its diff:
```python
import functools

import jax
import jax.numpy as jnp
from jax import lax
from jax.experimental import pallas as pl
from jax.experimental.pallas import tpu as pltpu
from jax.sharding import PartitionSpec as P

MESH = pl.DeviceIdType.MESH
NN = (((1,), (0,)), ((), ()))
NT = (((1,), (1,)), ((), ()))


def dot(a, b, dims):
    return lax.dot_general(a, b, dims, preferred_element_type=jnp.float32)


def kernel(
    chain,
    teams,
    chunks,
    potential,
    energies,
    weights,
    indices,
    levels,
    left_source,
    right_source,
    left_hbm,
    right_hbm,
    out,
    left,
    right,
    first,
    density,
    gathered,
    forward_in,
    forward_out,
    backward_in,
    backward_out,
    load_sem,
    forward_send,
    forward_recv,
    backward_send,
    backward_recv,
    gather_send,
    gather_recv,
):
    count = indices.shape[0]
    orbitals = levels.shape[1]
    modes = left_source.shape[1]
    width = orbitals // chunks
    spot = lax.axis_index("slab")
    team = lax.axis_index("energy")

    loads = [
        pltpu.make_async_copy(right_hbm.at[0], right, load_sem.at[0]),
        pltpu.make_async_copy(left_hbm.at[0], left, load_sem.at[1]),
    ]
    for load in loads:
        load.start()

    barrier = pltpu.get_barrier_semaphore()

    def greet(step):
        pl.semaphore_signal(barrier, inc=1, device_id={"slab": spot + step}, device_id_type=MESH)

    pl.when(spot > 0)(lambda: greet(-1))
    pl.when(spot < chain - 1)(lambda: greet(1))
    for step in range(1, teams):
        peer = lax.rem(team + step, teams)
        pl.semaphore_signal(barrier, inc=1, device_id={"energy": peer}, device_id_type=MESH)

    row = levels[pl.ds(potential[0], 1), :]
    density[...] = jnp.zeros_like(density)

    for load in loads:
        load.wait()

    @pl.when(spot == 0)
    def _():
        source = left_source[...].astype(jnp.float32).T.astype(jnp.bfloat16)
        first[...] = dot(source, right[...], NT)

    @pl.when(spot == chain - 1)
    def _():
        source = right_source[...].astype(jnp.float32).T.astype(jnp.bfloat16)
        first[...] = dot(source, left[...], NN)

    at_end = (spot == 0) | (spot == chain - 1)
    pl.when(at_end)(lambda: pl.semaphore_wait(barrier, teams))
    pl.when(jnp.logical_not(at_end))(lambda: pl.semaphore_wait(barrier, teams + 1))

    def copy_of(source, target, send, recv, slot, chunk, step):
        return pltpu.make_async_remote_copy(
            src_ref=source.at[slot, chunk],
            dst_ref=target.at[slot, chunk],
            send_sem=send.at[slot, chunk],
            recv_sem=recv.at[slot, chunk],
            device_id={"slab": spot + step},
            device_id_type=MESH,
        )

    forward_copy = functools.partial(
        copy_of, forward_out, forward_in, forward_send, forward_recv, step=1
    )
    backward_copy = functools.partial(
        copy_of, backward_out, backward_in, backward_send, backward_recv, step=-1
    )

    def work(slot, is_first, is_last, copy, state_in, state_out, mix, spread):
        scale = 1.0 / (energies[indices[slot]] - row)
        weight = weights[indices[slot]] / (count * teams * modes)

        def finish(mixed):
            scaled = (scale * mixed).astype(jnp.bfloat16)
            for chunk in range(chunks):
                fresh = spread(scaled, chunk).astype(jnp.bfloat16)
                state_out[slot, chunk] = fresh
                pl.when(jnp.logical_not(is_last))(lambda: copy(slot, chunk).start())
            for chunk in range(chunks):
                squared = state_out[slot, chunk].astype(jnp.float32) ** 2
                part = jnp.sum(squared.reshape(modes // 8, 8, width), axis=0)
                lanes = slice(chunk * width, (chunk + 1) * width)
                density[:, lanes] += weight * part

        @pl.when(is_first)
        def _():
            finish(first[...])

        @pl.when(jnp.logical_not(is_first))
        def _():
            mixed = None
            for chunk in range(chunks):
                copy(slot, chunk).wait_recv()
                part = mix(state_in[slot, chunk], chunk)
                mixed = part if mixed is None else mixed + part
            finish(mixed)

    def lanes_of(chunk):
        return slice(chunk * width, (chunk + 1) * width)

    def turn(time, carry):
        slot = time - spot

        @pl.when((slot >= 0) & (slot < count))
        def _():
            work(
                slot,
                spot == 0,
                spot == chain - 1,
                forward_copy,
                forward_in,
                forward_out,
                lambda state, chunk: dot(state, right[:, lanes_of(chunk)], NT),
                lambda scaled, chunk: dot(scaled, left[lanes_of(chunk), :], NT),
            )

        other = time - (chain - 1 - spot)

        @pl.when((other >= 0) & (other < count))
        def _():
            work(
                other,
                spot == chain - 1,
                spot == 0,
                backward_copy,
                backward_in,
                backward_out,
                lambda state, chunk: dot(state, left[lanes_of(chunk), :], NN),
                lambda scaled, chunk: dot(scaled, right[:, lanes_of(chunk)], NN),
            )

        return carry

    lax.fori_loop(0, chain + count - 1, turn, 0)

    gathered[team] = jnp.sum(density[...], axis=0, keepdims=True)

    def share(step):
        peer = lax.rem(team + step, teams)
        return pltpu.make_async_remote_copy(
            src_ref=gathered.at[team],
            dst_ref=gathered.at[team],
            send_sem=gather_send.at[step],
            recv_sem=gather_recv.at[step],
            device_id={"energy": peer},
            device_id_type=MESH,
        )

    for step in range(1, teams):
        share(step).start()

    def settle(slot, carry):
        for chunk in range(chunks):
            pl.when(spot < chain - 1)(lambda: forward_copy(slot, chunk).wait_send())
            pl.when(spot > 0)(lambda: backward_copy(slot, chunk).wait_send())
        return carry

    lax.fori_loop(0, count, settle, 0)
    for step in range(1, teams):
        share(step).wait()
    total = gathered[0]
    for member in range(1, teams):
        total += gathered[member]
    out[...] = total


def local(
    teams,
    chain,
    left_basis,
    right_basis,
    potential_index,
    levels,
    energy_values,
    energy_weights,
    energy_index,
    left_source,
    right_source,
):
    count = energy_index.shape[0]
    orbitals = left_basis.shape[1]
    modes = left_source.shape[1]
    chunks = 3 if orbitals % 384 == 0 else 1
    block = (count, chunks, modes, orbitals // chunks)
    scalars = pl.BlockSpec(memory_space=pltpu.SMEM)
    vectors = pl.BlockSpec(memory_space=pltpu.VMEM)
    outside = pl.BlockSpec(memory_space=pl.ANY)
    copies = pltpu.SemaphoreType.DMA((count, chunks))
    return pl.pallas_call(
        functools.partial(kernel, chain, teams, chunks),
        out_shape=jax.ShapeDtypeStruct((1, orbitals), jnp.float32),
        in_specs=[scalars] * 4 + [vectors] * 3 + [outside] * 2,
        out_specs=vectors,
        scratch_shapes=[
            pltpu.VMEM((orbitals, orbitals), jnp.bfloat16),
            pltpu.VMEM((orbitals, orbitals), jnp.bfloat16),
            pltpu.VMEM((modes, orbitals), jnp.float32),
            pltpu.VMEM((8, orbitals), jnp.float32),
            pltpu.VMEM((teams, 1, orbitals), jnp.float32),
            pltpu.VMEM(block, jnp.bfloat16),
            pltpu.VMEM(block, jnp.bfloat16),
            pltpu.VMEM(block, jnp.bfloat16),
            pltpu.VMEM(block, jnp.bfloat16),
            pltpu.SemaphoreType.DMA((2,)),
            copies,
            copies,
            copies,
            copies,
            pltpu.SemaphoreType.DMA((teams,)),
            pltpu.SemaphoreType.DMA((teams,)),
        ],
        compiler_params=pltpu.CompilerParams(
            collective_id=0, has_side_effects=True, vmem_limit_bytes=32 << 20
        ),
    )(
        potential_index,
        energy_values,
        energy_weights,
        energy_index,
        levels,
        left_source,
        right_source,
        left_basis,
        right_basis,
    )


def solution(mesh):
    placed = (
        P("slab", None, None),
        P("slab", None, None),
        P("slab"),
        P(),
        P(),
        P(),
        P("energy"),
        P(),
        P(),
    )
    return jax.shard_map(
        functools.partial(local, mesh.shape["energy"], mesh.shape["slab"]),
        mesh=mesh,
        in_specs=placed,
        out_specs=P("slab", None),
        check_vma=False,
    )
```

time: 215 us -> 51.9 us (0.24)
  the two profiles are of different devices: /device:TPU:24 before, /device:TPU:0 now
where the time goes in v1:
time: 51.9 us; the launch traced here: 51.5 us
  Pallas kernels  43.2 us (83%)
  local copies, waits for them, and re-layouts  7.67 us (15%)
  between operations  0.68 us (1%)
    pallas_call x1, Pallas kernels, local(): pl.pallas_call(functools.partial(kernel, chain, teams, chunks), out_shape...  43.2 us
    unnamed x17, local copies, waits for them, and re-layouts  7.67 us

profile of v1, /device:TPU:0, one launch (start us, length us, event | category | flops | bytes accessed | tf_op | source)
XLA Modules:
  0.0 51.5 jit_solution(10518774359126982323)
XLA Ops:
  0.7 0.0 copy-start
  0.7 1.3 %copy-done = bf16[1,768,768]{2,1,0:T(8,128)(2,1)S(1)} copy-done((bf16[1,768,768]{2,1,0:T(8,128)(2,1)S(1)}, bf16[1,768,768]{2,1,0:T(8,128)(2,1)}, u32[]{:S(2)}) %copy-start) | copy-done | bytes 1179672
  1.9 0.0 copy-start.1
  1.9 1.3 %copy-done.1 = bf16[1,768,768]{2,1,0:T(8,128)(2,1)S(1)} copy-done((bf16[1,768,768]{2,1,0:T(8,128)(2,1)S(1)}, bf16[1,768,768]{2,1,0:T(8,128)(2,1)}, u32[]{:S(2)}) %copy-start.1) | copy-done | bytes 1179672
  3.2 0.0 copy-start.2
  3.2 0.9 %copy-done.2 = bf16[768,128]{1,0:T(8,128)(2,1)S(1)} copy-done((bf16[768,128]{1,0:T(8,128)(2,1)S(1)}, bf16[768,128]{1,0:T(8,128)(2,1)}, u32[]{:S(2)}) %copy-start.2) | copy-done | bytes 196632
  4.1 0.0 copy-start.3
  4.1 0.9 %copy-done.3 = bf16[768,128]{1,0:T(8,128)(2,1)S(1)} copy-done((bf16[768,128]{1,0:T(8,128)(2,1)S(1)}, bf16[768,128]{1,0:T(8,128)(2,1)}, u32[]{:S(2)}) %copy-start.3) | copy-done | bytes 196632
  5.0 0.0 copy-start.4
  5.1 0.7 %copy-done.4 = f32[8,768]{1,0:T(8,128)S(1)} copy-done((f32[8,768]{1,0:T(8,128)S(1)}, f32[8,768]{1,0:T(8,128)}, u32[]{:S(2)}) %copy-start.4) | copy-done | bytes 24600
  5.8 0.0 copy-start.5
  5.8 0.7 %copy-done.5 = f32[64]{0:T(128)S(1)} copy-done((f32[64]{0:T(128)S(1)}, f32[64]{0:T(128)}, u32[]{:S(2)}) %copy-start.5) | copy-done | bytes 280
  6.4 0.0 copy-start.6
  6.4 0.7 %copy-done.6 = f32[64]{0:T(128)S(1)} copy-done((f32[64]{0:T(128)S(1)}, f32[64]{0:T(128)}, u32[]{:S(2)}) %copy-start.6) | copy-done | bytes 280
  7.1 0.0 copy-start.7
  7.1 0.7 %copy-done.7 = s32[4]{0:T(128)S(1)} copy-done((s32[4]{0:T(128)S(1)}, s32[4]{0:T(128)}, u32[]{:S(2)}) %copy-start.7) | copy-done | bytes 40
  7.8 43.2 %shard_map.91 = f32[1,768]{1,0:T(1,128)S(1)} custom-call(s32[1]{0:T(128)S(6)} %copy.11.potential, f32[64]{0:T(128)S(1)} %copy-done.5, f32[64]{0:T(128)S(1)} %copy-done.6, s32[4]{0:T(128)S(1)} %copy-done.7, f32[8,768]{1,0:T(8,128)S(1)} %copy-done.4, bf16[768,128]{1,0:T(8,128)(2,1)S(1)} %copy-done.2, bf16[768,128]{1,0:T(8,128)(2,1)S(1)} %copy-done.3, ...), custom_call_target="tpu_custom_call" | custom-call | tf_op jit(solution)/shard_map/pallas_call | solution.py:232
  50.9 0.6 %copy.12 = f32[1,768]{1,0:T(1,128)} copy(f32[1,768]{1,0:T(1,128)S(1)} %shard_map.91) | data formatting | bytes 6144
Async XLA Ops:
  0.7 1.3 %copy-start = (bf16[1,768,768]{2,1,0:T(8,128)(2,1)S(1)}, bf16[1,768,768]{2,1,0:T(8,128)(2,1)}, u32[]{:S(2)}) copy-start(bf16[1,768,768]{2,1,0:T(8,128)(2,1)} %left_hbm.1) | copy-start | bytes 3538948
  1.9 1.3 %copy-start.1 = (bf16[1,768,768]{2,1,0:T(8,128)(2,1)S(1)}, bf16[1,768,768]{2,1,0:T(8,128)(2,1)}, u32[]{:S(2)}) copy-start(bf16[1,768,768]{2,1,0:T(8,128)(2,1)} %right_hbm.1) | copy-start | bytes 3538948
  3.2 0.9 %copy-start.2 = (bf16[768,128]{1,0:T(8,128)(2,1)S(1)}, bf16[768,128]{1,0:T(8,128)(2,1)}, u32[]{:S(2)}) copy-start(bf16[768,128]{1,0:T(8,128)(2,1)} %left_source.1) | copy-start | bytes 589828
  4.1 0.9 %copy-start.3 = (bf16[768,128]{1,0:T(8,128)(2,1)S(1)}, bf16[768,128]{1,0:T(8,128)(2,1)}, u32[]{:S(2)}) copy-start(bf16[768,128]{1,0:T(8,128)(2,1)} %right_source.1) | copy-start | bytes 589828
  5.0 0.7 %copy-start.4 = (f32[8,768]{1,0:T(8,128)S(1)}, f32[8,768]{1,0:T(8,128)}, u32[]{:S(2)}) copy-start(f32[8,768]{1,0:T(8,128)} %levels.1) | copy-start | bytes 73732
  5.8 0.7 %copy-start.5 = (f32[64]{0:T(128)S(1)}, f32[64]{0:T(128)}, u32[]{:S(2)}) copy-start(f32[64]{0:T(128)} %energies.1) | copy-start | bytes 772
  6.4 0.7 %copy-start.6 = (f32[64]{0:T(128)S(1)}, f32[64]{0:T(128)}, u32[]{:S(2)}) copy-start(f32[64]{0:T(128)} %weights.1) | copy-start | bytes 772
  7.1 0.7 %copy-start.7 = (s32[4]{0:T(128)S(1)}, s32[4]{0:T(128)}, u32[]{:S(2)}) copy-start(s32[4]{0:T(128)} %indices.1) | copy-start | bytes 52

commit v2 on v1

--- a/solution.py
+++ b/solution.py
@@ -21,17 +21,24 @@
     teams,
     chunks,
     potential,
+    energies_hbm,
+    weights_hbm,
+    indices_hbm,
+    levels_hbm,
+    left_source_hbm,
+    right_source_hbm,
+    left_hbm,
+    right_hbm,
+    out,
     energies,
     weights,
     indices,
     levels,
-    left_source,
-    right_source,
-    left_hbm,
-    right_hbm,
-    out,
+    source,
     left,
     right,
+    left_turned,
+    right_turned,
     first,
     density,
     gathered,
@@ -49,17 +56,27 @@
 ):
     count = indices.shape[0]
     orbitals = levels.shape[1]
-    modes = left_source.shape[1]
+    modes = source.shape[1]
     width = orbitals // chunks
     spot = lax.axis_index("slab")
     team = lax.axis_index("energy")
 
-    loads = [
-        pltpu.make_async_copy(right_hbm.at[0], right, load_sem.at[0]),
-        pltpu.make_async_copy(left_hbm.at[0], left, load_sem.at[1]),
+    def load(origin, target, place):
+        return pltpu.make_async_copy(origin, target, load_sem.at[place])
+
+    left_load = load(left_source_hbm, source, 0)
+    right_load = load(right_source_hbm, source, 0)
+    bases = [load(right_hbm.at[0], right, 1), load(left_hbm.at[0], left, 2)]
+    tables = [
+        load(energies_hbm, energies, 4),
+        load(weights_hbm, weights, 5),
+        load(indices_hbm, indices, 6),
+        load(levels_hbm, levels, 7),
     ]
-    for load in loads:
-        load.start()
+    pl.when(spot == 0)(left_load.start)
+    pl.when(spot == chain - 1)(right_load.start)
+    for item in bases + tables:
+        item.start()
 
     barrier = pltpu.get_barrier_semaphore()
 
@@ -72,21 +89,33 @@
         peer = lax.rem(team + step, teams)
         pl.semaphore_signal(barrier, inc=1, device_id={"energy": peer}, device_id_type=MESH)
 
-    row = levels[pl.ds(potential[0], 1), :]
     density[...] = jnp.zeros_like(density)
-
-    for load in loads:
-        load.wait()
+    for item in bases:
+        item.wait()
+
+    def turned_source():
+        return source[...].astype(jnp.float32).T.astype(jnp.bfloat16)
 
     @pl.when(spot == 0)
     def _():
-        source = left_source[...].astype(jnp.float32).T.astype(jnp.bfloat16)
-        first[...] = dot(source, right[...], NT)
+        left_load.wait()
+        first[...] = dot(turned_source(), right[...], NT)
 
     @pl.when(spot == chain - 1)
     def _():
-        source = right_source[...].astype(jnp.float32).T.astype(jnp.bfloat16)
-        first[...] = dot(source, left[...], NN)
+        right_load.wait()
+        first[...] = dot(turned_source(), left[...], NN)
+
+    def turn_bases():
+        for chunk in range(chunks):
+            rows = slice(chunk * width, (chunk + 1) * width)
+            left_turned[rows, :] = left[:, rows].T
+            right_turned[rows, :] = right[:, rows].T
+
+    pl.when((spot > 0) & (spot < chain - 1))(turn_bases)
+    for item in tables:
+        item.wait()
+    row = levels[pl.ds(potential[0], 1), :]
 
     at_end = (spot == 0) | (spot == chain - 1)
     pl.when(at_end)(lambda: pl.semaphore_wait(barrier, teams))
@@ -109,11 +138,11 @@
         copy_of, backward_out, backward_in, backward_send, backward_recv, step=-1
     )
 
-    def work(slot, is_first, is_last, copy, state_in, state_out, mix, spread):
+    def work(slot, is_first, is_last, copy, state_in, state_out, mix, spread, first_spread):
         scale = 1.0 / (energies[indices[slot]] - row)
         weight = weights[indices[slot]] / (count * teams * modes)
 
-        def finish(mixed):
+        def finish(mixed, spread):
             scaled = (scale * mixed).astype(jnp.bfloat16)
             for chunk in range(chunks):
                 fresh = spread(scaled, chunk).astype(jnp.bfloat16)
@@ -127,7 +156,7 @@
 
         @pl.when(is_first)
         def _():
-            finish(first[...])
+            finish(first[...], first_spread)
 
         @pl.when(jnp.logical_not(is_first))
         def _():
@@ -136,12 +165,14 @@
                 copy(slot, chunk).wait_recv()
                 part = mix(state_in[slot, chunk], chunk)
                 mixed = part if mixed is None else mixed + part
-            finish(mixed)
+            finish(mixed, spread)
 
     def lanes_of(chunk):
         return slice(chunk * width, (chunk + 1) * width)
 
     def turn(time, carry):
+        idle = min(count, chain - 1)
+        pl.when((spot == chain - 1) & (time == idle))(turn_bases)
         slot = time - spot
 
         @pl.when((slot >= 0) & (slot < count))
@@ -153,7 +184,8 @@
                 forward_copy,
                 forward_in,
                 forward_out,
-                lambda state, chunk: dot(state, right[:, lanes_of(chunk)], NT),
+                lambda state, chunk: dot(state, right_turned[lanes_of(chunk), :], NN),
+                lambda scaled, chunk: dot(scaled, left_turned[:, lanes_of(chunk)], NN),
                 lambda scaled, chunk: dot(scaled, left[lanes_of(chunk), :], NT),
             )
 
@@ -169,6 +201,7 @@
                 backward_in,
                 backward_out,
                 lambda state, chunk: dot(state, left[lanes_of(chunk), :], NN),
+                lambda scaled, chunk: dot(scaled, right[:, lanes_of(chunk)], NN),
                 lambda scaled, chunk: dot(scaled, right[:, lanes_of(chunk)], NN),
             )
 
@@ -225,18 +258,24 @@
     modes = left_source.shape[1]
     chunks = 3 if orbitals % 384 == 0 else 1
     block = (count, chunks, modes, orbitals // chunks)
-    scalars = pl.BlockSpec(memory_space=pltpu.SMEM)
-    vectors = pl.BlockSpec(memory_space=pltpu.VMEM)
-    outside = pl.BlockSpec(memory_space=pl.ANY)
+    outside = pl.BlockSpec(memory_space=pltpu.HBM)
+    square = pltpu.VMEM((orbitals, orbitals), jnp.bfloat16)
     copies = pltpu.SemaphoreType.DMA((count, chunks))
     return pl.pallas_call(
         functools.partial(kernel, chain, teams, chunks),
         out_shape=jax.ShapeDtypeStruct((1, orbitals), jnp.float32),
-        in_specs=[scalars] * 4 + [vectors] * 3 + [outside] * 2,
-        out_specs=vectors,
+        in_specs=[pl.BlockSpec(memory_space=pltpu.SMEM)] + [outside] * 8,
+        out_specs=pl.BlockSpec(memory_space=pltpu.VMEM),
         scratch_shapes=[
-            pltpu.VMEM((orbitals, orbitals), jnp.bfloat16),
-            pltpu.VMEM((orbitals, orbitals), jnp.bfloat16),
+            pltpu.SMEM(energy_values.shape, jnp.float32),
+            pltpu.SMEM(energy_weights.shape, jnp.float32),
+            pltpu.SMEM(energy_index.shape, jnp.int32),
+            pltpu.VMEM(levels.shape, jnp.float32),
+            pltpu.VMEM(left_source.shape, jnp.bfloat16),
+            square,
+            square,
+            square,
+            square,
             pltpu.VMEM((modes, orbitals), jnp.float32),
             pltpu.VMEM((8, orbitals), jnp.float32),
             pltpu.VMEM((teams, 1, orbitals), jnp.float32),
@@ -244,7 +283,7 @@
             pltpu.VMEM(block, jnp.bfloat16),
             pltpu.VMEM(block, jnp.bfloat16),
             pltpu.VMEM(block, jnp.bfloat16),
-            pltpu.SemaphoreType.DMA((2,)),
+            pltpu.SemaphoreType.DMA((8,)),
             copies,
             copies,
             copies,
@@ -253,7 +292,7 @@
             pltpu.SemaphoreType.DMA((teams,)),
         ],
         compiler_params=pltpu.CompilerParams(
-            collective_id=0, has_side_effects=True, vmem_limit_bytes=32 << 20
+            collective_id=0, has_side_effects=True, vmem_limit_bytes=63 << 20
         ),
     )(
         potential_index,

time: 51.9 us -> 45.9 us (0.88)
  local copies, waits for them, and re-layouts: 7.67 us -> 1.26 us
  Pallas kernels: 43.2 us -> 43.8 us
    unnamed x17 -> x1, local copies, waits for them, and re-layouts: 7.67 us -> 1.26 us
    pallas_call x1, Pallas kernels: 43.2 us -> 43.8 us  [local(): pl.pallas_call(functools.partial(kernel, chain, teams, chunks), out_shape...]
where the time goes in v2:
time: 45.9 us; the launch traced here: 45.7 us
  Pallas kernels  43.8 us (95%)
  local copies, waits for them, and re-layouts  1.26 us (3%)
  between operations  0.66 us (1%)
    pallas_call x1, Pallas kernels, local(): pl.pallas_call(functools.partial(kernel, chain, teams, chunks), out_shape...  43.8 us
    unnamed x1, local copies, waits for them, and re-layouts  1.26 us

profile of v2, /device:TPU:0, one launch (start us, length us, event | category | flops | bytes accessed | tf_op | source)
XLA Modules:
  0.0 45.7 jit_solution(2309317438887136807)
XLA Ops:
  0.7 43.8 %shard_map.91 = f32[1,768]{1,0:T(1,128)} custom-call(s32[1]{0:T(128)S(6)} %copy.11.potential, f32[64]{0:T(128)} %energies_hbm.1, f32[64]{0:T(128)} %weights_hbm.1, s32[4]{0:T(128)} %indices_hbm.1, f32[8,768]{1,0:T(8,128)} %levels_hbm.1, bf16[768,128]{1,0:T(8,128)(2,1)} %left_source_hbm.1, bf16[768,128]{1,0:T(8,128)(2,1)} %right_source_hbm.1, ...), custom_call_target="tpu_custom_call" | custom-call | tf_op jit(solution)/shard_map/pallas_call | solution.py:264
  44.4 1.3 %copy.12 = f32[1,768]{1,0:T(1,128)} copy(f32[1,768]{1,0:T(1,128)} %shard_map.91) | data formatting | bytes 6144

commit v3 on v2

--- a/solution.py
+++ b/solution.py
@@ -90,8 +90,6 @@
         pl.semaphore_signal(barrier, inc=1, device_id={"energy": peer}, device_id_type=MESH)
 
     density[...] = jnp.zeros_like(density)
-    for item in bases:
-        item.wait()
 
     def turned_source():
         return source[...].astype(jnp.float32).T.astype(jnp.bfloat16)
@@ -99,11 +97,13 @@
     @pl.when(spot == 0)
     def _():
         left_load.wait()
+        bases[0].wait()
         first[...] = dot(turned_source(), right[...], NT)
 
     @pl.when(spot == chain - 1)
     def _():
         right_load.wait()
+        bases[1].wait()
         first[...] = dot(turned_source(), left[...], NN)
 
     def turn_bases():
@@ -112,7 +112,15 @@
             left_turned[rows, :] = left[:, rows].T
             right_turned[rows, :] = right[:, rows].T
 
-    pl.when((spot > 0) & (spot < chain - 1))(turn_bases)
+    pl.when(spot == 0)(bases[1].wait)
+    pl.when(spot == chain - 1)(bases[0].wait)
+
+    @pl.when((spot > 0) & (spot < chain - 1))
+    def _():
+        for item in bases:
+            item.wait()
+        turn_bases()
+
     for item in tables:
         item.wait()
     row = levels[pl.ds(potential[0], 1), :]
@@ -170,12 +178,10 @@
     def lanes_of(chunk):
         return slice(chunk * width, (chunk + 1) * width)
 
-    def turn(time, carry):
-        idle = min(count, chain - 1)
-        pl.when((spot == chain - 1) & (time == idle))(turn_bases)
+    def forward(time, wanted):
         slot = time - spot
 
-        @pl.when((slot >= 0) & (slot < count))
+        @pl.when(wanted & (slot >= 0) & (slot < count))
         def _():
             work(
                 slot,
@@ -189,6 +195,7 @@
                 lambda scaled, chunk: dot(scaled, left[lanes_of(chunk), :], NT),
             )
 
+    def backward(time):
         other = time - (chain - 1 - spot)
 
         @pl.when((other >= 0) & (other < count))
@@ -205,6 +212,12 @@
                 lambda scaled, chunk: dot(scaled, right[:, lanes_of(chunk)], NN),
             )
 
+    def turn(time, carry):
+        idle = min(count, chain - 1)
+        pl.when((spot == chain - 1) & (time == idle))(turn_bases)
+        forward(time, spot < chain // 2)
+        backward(time)
+        forward(time, spot >= chain // 2)
         return carry
 
     lax.fori_loop(0, chain + count - 1, turn, 0)
@@ -256,7 +269,7 @@
     count = energy_index.shape[0]
     orbitals = left_basis.shape[1]
     modes = left_source.shape[1]
-    chunks = 3 if orbitals % 384 == 0 else 1
+    chunks = 1
     block = (count, chunks, modes, orbitals // chunks)
     outside = pl.BlockSpec(memory_space=pltpu.HBM)
     square = pltpu.VMEM((orbitals, orbitals), jnp.bfloat16)

time: 45.9 us -> 40.5 us (0.88)
  Pallas kernels: 43.8 us -> 38.5 us
    pallas_call x1, Pallas kernels: 43.8 us -> 38.5 us  [local(): pl.pallas_call(functools.partial(kernel, chain, teams, chunks), out_shape...]
where the time goes in v3:
time: 40.5 us; the launch traced here: 40.4 us
  Pallas kernels  38.5 us (95%)
  local copies, waits for them, and re-layouts  1.26 us (3%)
  between operations  0.66 us (2%)
    pallas_call x1, Pallas kernels, local(): pl.pallas_call(functools.partial(kernel, chain, teams, chunks), out_shape...  38.5 us
    unnamed x1, local copies, waits for them, and re-layouts  1.26 us

profile of v3, /device:TPU:0, one launch (start us, length us, event | category | flops | bytes accessed | tf_op | source)
XLA Modules:
  0.0 40.4 jit_solution(4506963459165711697)
XLA Ops:
  0.7 38.5 %shard_map.91 = f32[1,768]{1,0:T(1,128)} custom-call(s32[1]{0:T(128)S(6)} %copy.11.potential, f32[64]{0:T(128)} %energies_hbm.1, f32[64]{0:T(128)} %weights_hbm.1, s32[4]{0:T(128)} %indices_hbm.1, f32[8,768]{1,0:T(8,128)} %levels_hbm.1, bf16[768,128]{1,0:T(8,128)(2,1)} %left_source_hbm.1, bf16[768,128]{1,0:T(8,128)(2,1)} %right_source_hbm.1, ...), custom_call_target="tpu_custom_call" | custom-call | tf_op jit(solution)/shard_map/pallas_call | solution.py:277
  39.1 1.3 %copy.12 = f32[1,768]{1,0:T(1,128)} copy(f32[1,768]{1,0:T(1,128)} %shard_map.91) | data formatting | bytes 6144

commit v4 on v2

v4 whole, which is shorter than its diff:
```python
import functools

import jax
import jax.numpy as jnp
from jax import lax
from jax.experimental import pallas as pl
from jax.experimental.pallas import tpu as pltpu
from jax.sharding import PartitionSpec as P

MESH = pl.DeviceIdType.MESH
NN = (((1,), (0,)), ((), ()))
NT = (((1,), (1,)), ((), ()))


def dot(a, b, dims):
    return lax.dot_general(a, b, dims, preferred_element_type=jnp.float32)


def kernel(
    chain,
    teams,
    potential,
    energies_hbm,
    weights_hbm,
    indices_hbm,
    levels_hbm,
    left_source_hbm,
    right_source_hbm,
    left_hbm,
    right_hbm,
    out,
    energies,
    weights,
    indices,
    levels,
    source,
    left,
    right,
    left_turned,
    right_turned,
    rows,
    first,
    middle,
    density,
    partial,
    gathered,
    forward_in,
    forward_out,
    backward_in,
    backward_out,
    load_sem,
    swap_send,
    swap_recv,
    forward_send,
    forward_recv,
    backward_send,
    backward_recv,
    gather_send,
    gather_recv,
):
    count = indices.shape[0]
    modes = source.shape[1]
    orbitals = levels.shape[1]
    spot = lax.axis_index("slab")
    team = lax.axis_index("energy")
    chips = chain // 2
    chip = spot // 2
    core = spot % 2
    twin = spot + 1 - 2 * core
    lowest = chip == 0
    highest = chip == chips - 1

    def load(origin, target, place):
        return pltpu.make_async_copy(origin, target, load_sem.at[place])

    left_load = load(left_source_hbm, source, 0)
    right_load = load(right_source_hbm, source, 0)
    bases = [
        load(right_hbm.at[0], right.at[core], 1),
        load(left_hbm.at[0], left.at[core], 2),
    ]
    tables = [
        load(energies_hbm, energies, 3),
        load(weights_hbm, weights, 4),
        load(indices_hbm, indices, 5),
        load(levels_hbm, levels, 6),
    ]
    pl.when(spot == 0)(left_load.start)
    pl.when(spot == chain - 1)(right_load.start)
    for item in bases + tables:
        item.start()

    barrier = pltpu.get_barrier_semaphore()

    def greet(place):
        pl.semaphore_signal(barrier, inc=1, device_id=place, device_id_type=MESH)

    def greet_chip(other):
        greet({"slab": 2 * other})
        greet({"slab": 2 * other + 1})

    pl.when(chip > 0)(lambda: greet_chip(chip - 1))
    pl.when(chip < chips - 1)(lambda: greet_chip(chip + 1))
    greet({"slab": twin})
    for step in range(1, teams):
        peer = lax.rem(team + step, teams)
        greet({"energy": peer})
        greet({"energy": peer, "slab": twin})

    density[...] = jnp.zeros_like(density)
    for item in tables:
        item.wait()
    rows[core] = levels[pl.ds(potential[0], 1), :]

    at_end = lowest | highest
    pl.when(at_end)(lambda: pl.semaphore_wait(barrier, 2 * teams + 1))
    pl.when(jnp.logical_not(at_end))(lambda: pl.semaphore_wait(barrier, 2 * teams + 3))

    def swap(origin, target, place):
        return pltpu.make_async_remote_copy(
            src_ref=origin,
            dst_ref=target,
            send_sem=swap_send.at[place],
            recv_sem=swap_recv.at[place],
            device_id={"slab": twin},
            device_id_type=MESH,
        )

    swaps = [
        swap(rows.at[core], rows.at[core], 0),
        swap(right_hbm.at[0], right.at[core], 1),
        swap(left_hbm.at[0], left.at[core], 2),
    ]
    for item in swaps:
        item.start()
    for item in bases:
        item.wait()

    def turned_source():
        return source[...].astype(jnp.float32).T.astype(jnp.bfloat16)

    @pl.when(spot == 0)
    def _():
        left_load.wait()
        first[...] = dot(turned_source(), right[0], NT)

    @pl.when(spot == chain - 1)
    def _():
        right_load.wait()
        first[...] = dot(turned_source(), left[1], NN)

    def turn_bases(side):
        left_turned[side] = left[side].T
        right_turned[side] = right[side].T

    def turn_both():
        turn_bases(0)
        turn_bases(1)

    def settle_swaps():
        for item in swaps:
            item.wait_recv()

    pl.when(spot == 1)(lambda: turn_bases(1))

    @pl.when(jnp.logical_not(at_end))
    def _():
        settle_swaps()
        turn_both()

    def copy_of(origin, target, send, recv, slot, place):
        return pltpu.make_async_remote_copy(
            src_ref=origin.at[slot],
            dst_ref=target.at[slot],
            send_sem=send.at[slot],
            recv_sem=recv.at[slot],
            device_id={"slab": place},
            device_id_type=MESH,
        )

    forward_copy = functools.partial(
        copy_of, forward_out, forward_in, forward_send, forward_recv
    )
    backward_copy = functools.partial(
        copy_of, backward_out, backward_in, backward_send, backward_recv
    )

    def scaled(mixed, slot, side):
        scale = 1.0 / (energies[indices[slot]] - rows[side])
        return (scale * mixed).astype(jnp.bfloat16)

    def count_in(state, slot, side):
        weight = weights[indices[slot]] / (count * teams * modes)
        squared = state[...].astype(jnp.float32) ** 2
        part = jnp.sum(squared.reshape(modes // 8, 8, orbitals), axis=0)
        density[side] += weight * part

    def down(state, slot, side):
        mixed = dot(state, right_turned[side], NN)
        return dot(scaled(mixed, slot, side), left_turned[side], NN).astype(jnp.bfloat16)

    def up(state, slot, side):
        mixed = dot(state, left[side], NN)
        return dot(scaled(mixed, slot, side), right[side], NN).astype(jnp.bfloat16)

    def each(body):
        def step(slot, carry):
            body(slot)
            return carry

        lax.fori_loop(0, count, step, 0)

    def mine(body):
        each(lambda slot: pl.when(slot % 2 == core)(lambda: body(slot)))

    def sweep(begin, end, near, far, copy, state_in, state_out, advance, opening, start, onward):
        @pl.when(begin & (core == near))
        def _():
            def body(slot):
                mixed = scaled(first[...], slot, near)
                state_out[slot] = opening(mixed).astype(jnp.bfloat16)
                copy(slot, twin).start()
                count_in(state_out.at[slot], slot, near)

            each(body)

        @pl.when(begin & (core == far))
        def _():
            def body(slot):
                copy(slot, twin).wait_recv()
                state_out[slot] = advance(state_in[slot], slot, far)
                copy(slot, start + slot % 2).start()
                count_in(state_out.at[slot], slot, far)

            each(body)

        @pl.when(jnp.logical_not(begin))
        def _():
            def body(slot):
                copy(slot, twin).wait_recv()
                middle[...] = advance(state_in[slot], slot, near)
                state_out[slot] = advance(middle[...], slot, far)
                pl.when(jnp.logical_not(end))(lambda: copy(slot, onward).start())
                count_in(middle, slot, near)
                count_in(state_out.at[slot], slot, far)

            mine(body)

    def forward():
        sweep(
            lowest, highest, 0, 1, forward_copy, forward_in, forward_out, down,
            lambda mixed: dot(mixed, left[0], NT), 2, spot + 2,
        )

    def backward():
        sweep(
            highest, lowest, 1, 0, backward_copy, backward_in, backward_out, up,
            lambda mixed: dot(mixed, right[1], NN), chain - 4, spot - 2,
        )

    upper = chip >= chips // 2
    pl.when(jnp.logical_not(upper))(forward)
    pl.when(lowest)(settle_swaps)
    backward()

    @pl.when(highest)
    def _():
        settle_swaps()
        turn_both()

    pl.when(upper)(forward)

    gathered[2 * team + core] = jnp.sum(density[core], axis=0, keepdims=True)
    partial[...] = jnp.sum(density[1 - core], axis=0, keepdims=True)

    def share(step, across):
        peer = lax.rem(team + step, teams)
        place = teams * across + step
        return pltpu.make_async_remote_copy(
            src_ref=partial if across else gathered.at[2 * team + core],
            dst_ref=gathered.at[2 * team + core],
            send_sem=gather_send.at[place],
            recv_sem=gather_recv.at[place],
            device_id={"energy": peer, "slab": twin if across else spot},
            device_id_type=MESH,
        )

    shares = [share(step, 1) for step in range(teams)]
    shares += [share(step, 0) for step in range(1, teams)]
    for item in shares:
        item.start()

    def sent(copy, begin, end):
        pl.when(begin)(lambda: each(lambda slot: copy(slot, twin).wait_send()))
        pl.when(jnp.logical_not(begin | end))(
            lambda: mine(lambda slot: copy(slot, twin).wait_send())
        )

    sent(forward_copy, lowest, highest)
    sent(backward_copy, highest, lowest)
    for item in swaps:
        item.wait_send()
    for item in shares:
        item.wait()
    total = gathered[0]
    for member in range(1, 2 * teams):
        total += gathered[member]
    out[...] = total


def local(
    teams,
    chain,
    left_basis,
    right_basis,
    potential_index,
    levels,
    energy_values,
    energy_weights,
    energy_index,
    left_source,
    right_source,
):
    count = energy_index.shape[0]
    orbitals = left_basis.shape[1]
    modes = left_source.shape[1]
    block = (count, modes, orbitals)
    outside = pl.BlockSpec(memory_space=pltpu.HBM)
    square = pltpu.VMEM((2, orbitals, orbitals), jnp.bfloat16)
    copies = pltpu.SemaphoreType.DMA((count,))
    return pl.pallas_call(
        functools.partial(kernel, chain, teams),
        out_shape=jax.ShapeDtypeStruct((1, orbitals), jnp.float32),
        in_specs=[pl.BlockSpec(memory_space=pltpu.SMEM)] + [outside] * 8,
        out_specs=pl.BlockSpec(memory_space=pltpu.VMEM),
        scratch_shapes=[
            pltpu.SMEM(energy_values.shape, jnp.float32),
            pltpu.SMEM(energy_weights.shape, jnp.float32),
            pltpu.SMEM(energy_index.shape, jnp.int32),
            pltpu.VMEM(levels.shape, jnp.float32),
            pltpu.VMEM(left_source.shape, jnp.bfloat16),
            square,
            square,
            square,
            square,
            pltpu.VMEM((2, 1, orbitals), jnp.float32),
            pltpu.VMEM((modes, orbitals), jnp.float32),
            pltpu.VMEM((modes, orbitals), jnp.bfloat16),
            pltpu.VMEM((2, 8, orbitals), jnp.float32),
            pltpu.VMEM((1, orbitals), jnp.float32),
            pltpu.VMEM((2 * teams, 1, orbitals), jnp.float32),
            pltpu.VMEM(block, jnp.bfloat16),
            pltpu.VMEM(block, jnp.bfloat16),
            pltpu.VMEM(block, jnp.bfloat16),
            pltpu.VMEM(block, jnp.bfloat16),
            pltpu.SemaphoreType.DMA((7,)),
            pltpu.SemaphoreType.DMA((3,)),
            pltpu.SemaphoreType.DMA((3,)),
            copies,
            copies,
            copies,
            copies,
            pltpu.SemaphoreType.DMA((2 * teams,)),
            pltpu.SemaphoreType.DMA((2 * teams,)),
        ],
        compiler_params=pltpu.CompilerParams(
            collective_id=0, has_side_effects=True, vmem_limit_bytes=63 << 20
        ),
    )(
        potential_index,
        energy_values,
        energy_weights,
        energy_index,
        levels,
        left_source,
        right_source,
        left_basis,
        right_basis,
    )


def solution(mesh):
    placed = (
        P("slab", None, None),
        P("slab", None, None),
        P("slab"),
        P(),
        P(),
        P(),
        P("energy"),
        P(),
        P(),
    )
    return jax.shard_map(
        functools.partial(local, mesh.shape["energy"], mesh.shape["slab"]),
        mesh=mesh,
        in_specs=placed,
        out_specs=P("slab", None),
        check_vma=False,
    )
```

time: 45.9 us -> 38.7 us (0.84)
  Pallas kernels: 43.8 us -> 36.6 us
    pallas_call x1, Pallas kernels: 43.8 us -> 36.6 us  [local(): pl.pallas_call(functools.partial(kernel, chain, teams), out_shape=jax.Sha...]
where the time goes in v4:
time: 38.7 us; the launch traced here: 38.5 us
  Pallas kernels  36.6 us (95%)
  local copies, waits for them, and re-layouts  1.26 us (3%)
  between operations  0.66 us (2%)
    pallas_call x1, Pallas kernels, local(): pl.pallas_call(functools.partial(kernel, chain, teams), out_shape=jax.Sha...  36.6 us
    unnamed x1, local copies, waits for them, and re-layouts  1.26 us

profile of v4, /device:TPU:0, one launch (start us, length us, event | category | flops | bytes accessed | tf_op | source)
XLA Modules:
  0.0 38.5 jit_solution(12076956345261883183)
XLA Ops:
  0.7 36.6 %shard_map.91 = f32[1,768]{1,0:T(1,128)} custom-call(s32[1]{0:T(128)S(6)} %copy.11.potential, f32[64]{0:T(128)} %energies_hbm.1, f32[64]{0:T(128)} %weights_hbm.1, s32[4]{0:T(128)} %indices_hbm.1, f32[8,768]{1,0:T(8,128)} %levels_hbm.1, bf16[768,128]{1,0:T(8,128)(2,1)} %left_source_hbm.1, bf16[768,128]{1,0:T(8,128)(2,1)} %right_source_hbm.1, ...), custom_call_target="tpu_custom_call" | custom-call | tf_op jit(solution)/shard_map/pallas_call | solution.py:331
  37.3 1.3 %copy.12 = f32[1,768]{1,0:T(1,128)} copy(f32[1,768]{1,0:T(1,128)} %shard_map.91) | data formatting | bytes 6144

commit v5 on v4

--- a/solution.py
+++ b/solution.py
@@ -113,8 +113,6 @@
     rows[core] = levels[pl.ds(potential[0], 1), :]
 
     at_end = lowest | highest
-    pl.when(at_end)(lambda: pl.semaphore_wait(barrier, 2 * teams + 1))
-    pl.when(jnp.logical_not(at_end))(lambda: pl.semaphore_wait(barrier, 2 * teams + 3))
 
     def swap(origin, target, place):
         return pltpu.make_async_remote_copy(
@@ -131,13 +129,26 @@
         swap(right_hbm.at[0], right.at[core], 1),
         swap(left_hbm.at[0], left.at[core], 2),
     ]
-    for item in swaps:
-        item.start()
-    for item in bases:
-        item.wait()
+    def settle_bases():
+        for item in bases:
+            item.wait()
+
+    def start_swaps():
+        for item in swaps:
+            item.start()
+
+    def settle_swaps():
+        for item in swaps:
+            item.wait_recv()
 
     def turned_source():
         return source[...].astype(jnp.float32).T.astype(jnp.bfloat16)
+
+    def turn_bases(side):
+        left_turned[side] = left[side].T
+        right_turned[side] = right[side].T
+
+    pl.when(at_end)(settle_bases)
 
     @pl.when(spot == 0)
     def _():
@@ -149,24 +160,18 @@
         right_load.wait()
         first[...] = dot(turned_source(), left[1], NN)
 
-    def turn_bases(side):
-        left_turned[side] = left[side].T
-        right_turned[side] = right[side].T
-
-    def turn_both():
-        turn_bases(0)
-        turn_bases(1)
-
-    def settle_swaps():
-        for item in swaps:
-            item.wait_recv()
-
     pl.when(spot == 1)(lambda: turn_bases(1))
+
+    pl.when(at_end)(lambda: pl.semaphore_wait(barrier, 2 * teams + 1))
+    pl.when(jnp.logical_not(at_end))(lambda: pl.semaphore_wait(barrier, 2 * teams + 3))
 
     @pl.when(jnp.logical_not(at_end))
     def _():
+        start_swaps()
+        settle_bases()
+        turn_bases(core)
         settle_swaps()
-        turn_both()
+        turn_bases(1 - core)
 
     def copy_of(origin, target, send, recv, slot, place):
         return pltpu.make_async_remote_copy(
@@ -260,13 +265,20 @@
 
     upper = chip >= chips // 2
     pl.when(jnp.logical_not(upper))(forward)
-    pl.when(lowest)(settle_swaps)
+
+    @pl.when(lowest)
+    def _():
+        start_swaps()
+        settle_swaps()
+
     backward()
 
     @pl.when(highest)
     def _():
+        start_swaps()
         settle_swaps()
-        turn_both()
+        turn_bases(0)
+        turn_bases(1)
 
     pl.when(upper)(forward)
 

time: 38.7 us -> 38.4 us (level)
  no operation moved by 1% of the time
where the time goes in v5:
time: 38.4 us; the launch traced here: 38.2 us
  Pallas kernels  36.3 us (95%)
  local copies, waits for them, and re-layouts  1.26 us (3%)
  between operations  0.66 us (2%)
    pallas_call x1, Pallas kernels, local(): pl.pallas_call(functools.partial(kernel, chain, teams), out_shape=jax.Sha...  36.3 us
    unnamed x1, local copies, waits for them, and re-layouts  1.26 us

profile of v5, /device:TPU:0, one launch (start us, length us, event | category | flops | bytes accessed | tf_op | source)
XLA Modules:
  0.0 38.2 jit_solution(98882173980431077)
XLA Ops:
  0.7 36.3 %shard_map.91 = f32[1,768]{1,0:T(1,128)} custom-call(s32[1]{0:T(128)S(6)} %copy.11.potential, f32[64]{0:T(128)} %energies_hbm.1, f32[64]{0:T(128)} %weights_hbm.1, s32[4]{0:T(128)} %indices_hbm.1, f32[8,768]{1,0:T(8,128)} %levels_hbm.1, bf16[768,128]{1,0:T(8,128)(2,1)} %left_source_hbm.1, bf16[768,128]{1,0:T(8,128)(2,1)} %right_source_hbm.1, ...), custom_call_target="tpu_custom_call" | custom-call | tf_op jit(solution)/shard_map/pallas_call | solution.py:343
  37.0 1.3 %copy.12 = f32[1,768]{1,0:T(1,128)} copy(f32[1,768]{1,0:T(1,128)} %shard_map.91) | data formatting | bytes 6144

commit v6 on v5

--- a/solution.py
+++ b/solution.py
@@ -244,9 +244,9 @@
             def body(slot):
                 copy(slot, twin).wait_recv()
                 middle[...] = advance(state_in[slot], slot, near)
+                count_in(middle, slot, near)
                 state_out[slot] = advance(middle[...], slot, far)
                 pl.when(jnp.logical_not(end))(lambda: copy(slot, onward).start())
-                count_in(middle, slot, near)
                 count_in(state_out.at[slot], slot, far)
 
             mine(body)

time: 38.4 us -> 38.3 us (level)
  no operation moved by 1% of the time
where the time goes in v6:
time: 38.3 us; the launch traced here: 38.2 us
  Pallas kernels  36.2 us (95%)
  local copies, waits for them, and re-layouts  1.26 us (3%)
  between operations  0.66 us (2%)
    pallas_call x1, Pallas kernels, local(): pl.pallas_call(functools.partial(kernel, chain, teams), out_shape=jax.Sha...  36.2 us
    unnamed x1, local copies, waits for them, and re-layouts  1.26 us

profile of v6, /device:TPU:0, one launch (start us, length us, event | category | flops | bytes accessed | tf_op | source)
XLA Modules:
  0.0 38.2 jit_solution(13481956529311958638)
XLA Ops:
  0.7 36.2 %shard_map.91 = f32[1,768]{1,0:T(1,128)} custom-call(s32[1]{0:T(128)S(6)} %copy.11.potential, f32[64]{0:T(128)} %energies_hbm.1, f32[64]{0:T(128)} %weights_hbm.1, s32[4]{0:T(128)} %indices_hbm.1, f32[8,768]{1,0:T(8,128)} %levels_hbm.1, bf16[768,128]{1,0:T(8,128)(2,1)} %left_source_hbm.1, bf16[768,128]{1,0:T(8,128)(2,1)} %right_source_hbm.1, ...), custom_call_target="tpu_custom_call" | custom-call | tf_op jit(solution)/shard_map/pallas_call | solution.py:343
  36.9 1.3 %copy.12 = f32[1,768]{1,0:T(1,128)} copy(f32[1,768]{1,0:T(1,128)} %shard_map.91) | data formatting | bytes 6144
